TPU v7x, 32 devices: a whole 2x2x4 slice. The times are simulated.
32 devices in a mesh: fsdp: 2 (over x), ctx: 4 (over y, core), tp: 4 (over z).
Axes of the slice: x: 2, y: 2, z: 4, core: 2. Of those that a mesh axis runs over, the one named last changes fastest.
Arguments:
- block_in: bfloat16 [8, 1024, 2048], P('fsdp', 'ctx', 'tp'), may hold values from -6 to 6
- seg_ids: int32 [8, 1024], P('fsdp'), may hold values from 0 to 7, never falling along the last dimension, each value on 1 to 512 neighbouring positions
- out_cot: bfloat16 [8, 1024, 2048], P('fsdp', 'ctx'), may hold values from -6 to 6
- norm_gain: bfloat16 [2048], P('tp'), may hold values from 0.099609375 to 1.8984375
- mid_gain: bfloat16 [2048], P('tp'), may hold values from 0.099609375 to 1.8984375
- gelu_proj: bfloat16 [2048, 2816], P(('fsdp', 'ctx'), 'tp'), may hold values from -0.125 to 0.125
- scan_proj: bfloat16 [2048, 2816], P(('fsdp', 'ctx'), 'tp'), may hold values from -0.125 to 0.125
- out_proj: bfloat16 [2816, 2048], P('tp', ('fsdp', 'ctx')), may hold values from -0.4375 to 0.4375
- gate_proj: bfloat16 [2048, 6144], P(('fsdp', 'ctx'), 'tp'), may hold values from -0.125 to 0.125
- up_proj: bfloat16 [2048, 6144], P(('fsdp', 'ctx'), 'tp'), may hold values from -0.125 to 0.125
- down_proj: bfloat16 [6144, 2048], P('tp', ('fsdp', 'ctx')), may hold values from -0.109375 to 0.109375
- conv_kernel: float32 [4, 2816], P(None, 'tp'), may hold values from -3 to 3
- conv_bias: float32 [2816], P('tp'), may hold values from -3 to 3
- rate_gate: bfloat16 [16, 176, 176], P('tp'), may hold values from -0.4375 to 0.4375
- input_gate: bfloat16 [16, 176, 176], P('tp'), may hold values from -0.4375 to 0.4375
- rate_bias: float32 [2816], P('tp'), may hold values from -4 to 4
- input_bias: float32 [2816], P('tp'), may hold values from -4 to 4
- decay_param: float32 [2816], P('tp'), may hold values from -16 to -4
Outputs:
- block_out: bfloat16 [8, 1024, 2048], P('fsdp', 'ctx', 'tp')
- grad_in: float32 [8, 1024, 2048], P('fsdp', 'ctx', 'tp')
- grad_norm_gain: float32 [2048], P('tp')
- grad_mid_gain: float32 [2048], P('tp')
- grad_gelu_proj: float32 [2048, 2816], P(('fsdp', 'ctx'), 'tp')
- grad_scan_proj: float32 [2048, 2816], P(('fsdp', 'ctx'), 'tp')
- grad_out_proj: float32 [2816, 2048], P('tp', ('fsdp', 'ctx'))
- grad_gate_proj: float32 [2048, 6144], P(('fsdp', 'ctx'), 'tp')
- grad_up_proj: float32 [2048, 6144], P(('fsdp', 'ctx'), 'tp')
- grad_down_proj: float32 [6144, 2048], P('tp', ('fsdp', 'ctx'))
- grad_conv_kernel: float32 [4, 2816], P(None, 'tp')
- grad_conv_bias: float32 [2816], P('tp')
- grad_rate_gate: float32 [16, 176, 176], P('tp')
- grad_input_gate: float32 [16, 176, 176], P('tp')
- grad_rate_bias: float32 [2816], P('tp')
- grad_input_bias: float32 [2816], P('tp')
- grad_decay_param: float32 [2816], P('tp')
Inputs may be any that keep to these rules, and one draw needn't show every extreme that they name: `seg_ids`: in every row the document numbers never fall; each of the 8 documents covers 1 to 512 positions, and one covers exactly 512.
All inputs are finite; a program needn't handle non-finite values.
Results may differ from a plain program's by a relative error of at most 0.0095.
Values may be sent and summed in bfloat16 or wider, within the bound.
A program may use at most 320 MiB of HBM per device.

v0:
```python
import jax
import jax.numpy as jnp
from jax import lax
from jax.sharding import PartitionSpec as P

CONV = 4
eps_norm = 1e-06


def from_behind(value, axis, steps):
    count = lax.axis_size(axis)
    leading, last = (max(0, -steps), min(count, count - steps))
    return lax.ppermute(value, axis, [(source, source + steps) for source in range(leading, last)])


def entering(value, axis, join, neutral, backward):
    count, mine = (lax.axis_size(axis), lax.axis_index(axis))
    pieces = jax.tree.map(lambda part: lax.all_gather(part, axis), value)
    if backward:
        pieces = jax.tree.map(lambda part: part[::-1], pieces)
        mine = count - 1 - mine
    total = jax.tree.map(
        lambda part, zero: jnp.full_like(part, 0) + jnp.asarray(zero, part.dtype), value, neutral
    )

    def step(position, total):
        longer = join(total, jax.tree.map(lambda part: part[position], pieces))
        return jax.tree.map(lambda new, old: jnp.where(position < mine, new, old), longer, total)

    return lax.fori_loop(0, count - 1, step, total)


def rms_scale(values, gain_vec):
    return (
        values * lax.rsqrt(jnp.mean(values * values, axis=-1, keepdims=True) + eps_norm) * gain_vec
    )


def gelu_tanh(values):
    return jax.nn.gelu(values, approximate=True)


def gate_values(pre_rate, pre_input, decay_param):
    rate_vals = jax.nn.sigmoid(pre_rate)
    input_vals = jax.nn.sigmoid(pre_input)
    log_a = -8.0 * jax.nn.softplus(decay_param) * rate_vals
    return (jnp.exp(log_a), jnp.sqrt(-jnp.expm1(2.0 * log_a)) * input_vals)


def combine(first_part, second_part):
    return (first_part[0] * second_part[0], second_part[0] * first_part[1] + second_part[1])


def matmul(left, right):
    return jnp.dot(left, right, preferred_element_type=jnp.float32)


def matmul_rt(left, right):
    return lax.dot_general(
        left, right, (((1,), (1,)), ((), ())), preferred_element_type=jnp.float32
    )


def matmul_lt(left, right):
    return lax.dot_general(
        left, right, (((0,), (0,)), ((), ())), preferred_element_type=jnp.float32
    )


def shards(
    block_in,
    seg_ids,
    out_cot,
    norm_gain,
    mid_gain,
    gelu_proj,
    scan_proj,
    out_proj,
    gate_proj,
    up_proj,
    down_proj,
    conv_kernel,
    conv_bias,
    rate_gate,
    input_gate,
    rate_bias,
    input_bias,
    decay_param,
):
    seq_count, tok_count, part_width = block_in.shape
    row_count = seq_count * tok_count
    full_in, gain_one, gain_two = (
        lax.all_gather(block_in, "tp", axis=2, tiled=True),
        lax.all_gather(norm_gain, "tp", axis=0, tiled=True),
        lax.all_gather(mid_gain, "tp", axis=0, tiled=True),
    )
    w_gelu, w_scan, w_out, w_gate, w_up, w_down = (
        lax.all_gather(gelu_proj, ("fsdp", "ctx"), axis=0, tiled=True),
        lax.all_gather(scan_proj, ("fsdp", "ctx"), axis=0, tiled=True),
        lax.all_gather(out_proj, ("fsdp", "ctx"), axis=1, tiled=True),
        lax.all_gather(gate_proj, ("fsdp", "ctx"), axis=0, tiled=True),
        lax.all_gather(up_proj, ("fsdp", "ctx"), axis=0, tiled=True),
        lax.all_gather(down_proj, ("fsdp", "ctx"), axis=1, tiled=True),
    )
    full_width = full_in.shape[2]
    rec_width = w_gelu.shape[1]
    head_count = rate_gate.shape[0]
    head_size = rate_gate.shape[1]
    x_rows = full_in.reshape(row_count, full_width).astype(jnp.float32)
    normed_f, norm_one_back = jax.vjp(rms_scale, x_rows, gain_one.astype(jnp.float32))
    normed = normed_f.astype(jnp.bfloat16)
    y_pre = matmul(normed, w_gelu)
    y_act, y_back = jax.vjp(gelu_tanh, y_pre)
    x_branch = matmul(normed, w_scan).astype(jnp.bfloat16).reshape(seq_count, tok_count, rec_width)
    margin_len = CONV - 1
    start_tok = lax.axis_index("ctx") * tok_count
    padded_ids = jnp.concatenate(
        [
            jnp.full((seq_count, margin_len), -1, jnp.int32),
            seg_ids,
            jnp.full((seq_count, margin_len), -2, jnp.int32),
        ],
        axis=1,
    )
    window_ids = lax.dynamic_slice_in_dim(padded_ids, start_tok, tok_count + 2 * margin_len, 1)
    own_ids = window_ids[:, margin_len : margin_len + tok_count]
    back_masks = [
        (window_ids[:, margin_len - offset : margin_len - offset + tok_count] == own_ids).astype(
            jnp.float32
        )[..., None]
        for offset in range(CONV)
    ]
    ahead_masks = [
        (window_ids[:, margin_len + offset : margin_len + offset + tok_count] == own_ids).astype(
            jnp.float32
        )[..., None]
        for offset in range(CONV)
    ]
    prev_edge = from_behind(x_branch[:, tok_count - margin_len :, :], "ctx", 1)
    ext_x = jnp.concatenate([prev_edge, x_branch], axis=1)
    conv_sum = conv_bias + jnp.zeros((seq_count, tok_count, rec_width), jnp.float32)
    for offset in range(CONV):
        conv_sum = (
            conv_sum
            + conv_kernel[offset]
            * ext_x[:, margin_len - offset : margin_len - offset + tok_count].astype(jnp.float32)
            * back_masks[offset]
        )
    conv_out = conv_sum.astype(jnp.bfloat16)
    conv_vals = conv_out.astype(jnp.float32)
    heads_in = conv_out.reshape(row_count, head_count, head_size)
    pre_rate = (
        jnp.einsum("rhi,hij->rhj", heads_in, rate_gate, preferred_element_type=jnp.float32).reshape(
            row_count, rec_width
        )
        + rate_bias
    )
    pre_input = (
        jnp.einsum(
            "rhi,hij->rhj", heads_in, input_gate, preferred_element_type=jnp.float32
        ).reshape(row_count, rec_width)
        + input_bias
    )
    (decays, in_scale), gate_back = jax.vjp(gate_values, pre_rate, pre_input, decay_param)
    in_scale3 = in_scale.reshape(seq_count, tok_count, rec_width)
    coeffs = decays.reshape(seq_count, tok_count, rec_width) * back_masks[1]
    inputs = in_scale3 * conv_vals
    cum_coef, local_state = lax.associative_scan(combine, (coeffs, inputs), axis=1)
    ones_row = jnp.ones((seq_count, rec_width), jnp.float32)
    zeros_row = jnp.zeros((seq_count, rec_width), jnp.float32)
    _, state_in = entering(
        (cum_coef[:, -1], local_state[:, -1]), "ctx", combine, (ones_row, zeros_row), False
    )
    states = local_state + cum_coef * state_in[:, None, :]
    state_rows = states.reshape(row_count, rec_width)
    mixed_in = (state_rows * y_act).astype(jnp.bfloat16)
    rec_part = matmul(mixed_in, w_out)
    col_start = lax.axis_index("tp") * part_width
    rec_total = lax.psum(rec_part, "tp")
    mid_rows = x_rows + rec_total
    normed_mid_f, norm_two_back = jax.vjp(rms_scale, mid_rows, gain_two.astype(jnp.float32))
    normed_mid = normed_mid_f.astype(jnp.bfloat16)
    gate_pre = matmul(normed_mid, w_gate)
    up_pre = matmul(normed_mid, w_up)
    gate_act, gate_act_back = jax.vjp(gelu_tanh, gate_pre)
    hidden = (gate_act * up_pre).astype(jnp.bfloat16)
    mlp_slice = lax.psum_scatter(matmul(hidden, w_down), "tp", scatter_dimension=1, tiled=True)
    mid_own = lax.dynamic_slice_in_dim(mid_rows, col_start, part_width, 1)
    block_out = (mid_own + mlp_slice).astype(jnp.bfloat16).reshape(seq_count, tok_count, part_width)
    cot_rows = out_cot.reshape(row_count, full_width)
    hid_grad = matmul_rt(cot_rows, w_down)
    grad_down = matmul_lt(hidden, cot_rows)
    gate_grad = gate_act_back(hid_grad * up_pre)[0].astype(jnp.bfloat16)
    up_grad = (hid_grad * gate_act).astype(jnp.bfloat16)
    grad_gate = matmul_lt(normed_mid, gate_grad)
    grad_up = matmul_lt(normed_mid, up_grad)
    mid_part = matmul_rt(gate_grad, w_gate) + matmul_rt(up_grad, w_up)
    mid_norm_grad = lax.psum(mid_part, "tp")
    mid_from_norm, gain_two_grad = norm_two_back(mid_norm_grad)
    mid_grad = cot_rows.astype(jnp.float32) + mid_from_norm
    rec_grad = mid_grad.astype(jnp.bfloat16)
    mixed_grad = matmul_rt(rec_grad, w_out)
    grad_out = matmul_lt(mixed_in, rec_grad)
    state_direct = (mixed_grad * y_act).reshape(seq_count, tok_count, rec_width)
    y_grad = y_back(mixed_grad * state_rows)[0].astype(jnp.bfloat16)
    grad_gelu = matmul_lt(normed, y_grad)
    in_part = matmul_rt(y_grad, w_gelu)
    next_coef = jnp.concatenate(
        [coeffs[:, 1:], jnp.ones((seq_count, 1, rec_width), jnp.float32)], axis=1
    )
    tail_coef, local_grad = lax.associative_scan(
        combine, (next_coef, state_direct), reverse=True, axis=1
    )
    head_coef = coeffs[:, 0]
    _, grad_in_state = entering(
        (head_coef * tail_coef[:, 0], head_coef * local_grad[:, 0]),
        "ctx",
        combine,
        (ones_row, zeros_row),
        True,
    )
    state_grad = local_grad + tail_coef * grad_in_state[:, None, :]
    prev_states = jnp.concatenate([state_in[:, None, :], states[:, :-1]], axis=1)
    decay_grad = (state_grad * prev_states * back_masks[1]).reshape(row_count, rec_width)
    scale_grad = (state_grad * conv_vals).reshape(row_count, rec_width)
    conv_direct = (state_grad * in_scale3).reshape(row_count, rec_width)
    rate_raw, input_raw, grad_decay = gate_back((decay_grad, scale_grad))
    rate_grad = rate_raw.astype(jnp.bfloat16)
    input_grad = input_raw.astype(jnp.bfloat16)
    rate_heads = rate_grad.reshape(row_count, head_count, head_size)
    input_heads = input_grad.reshape(row_count, head_count, head_size)
    grad_rate_gate = jnp.einsum(
        "rhi,rhj->hij", heads_in, rate_heads, preferred_element_type=jnp.float32
    )
    grad_input_gate = jnp.einsum(
        "rhi,rhj->hij", heads_in, input_heads, preferred_element_type=jnp.float32
    )
    grad_rate_bias = jnp.sum(rate_grad.astype(jnp.float32), axis=0)
    grad_input_bias = jnp.sum(input_grad.astype(jnp.float32), axis=0)
    gate_back_in = jnp.einsum(
        "rhj,hij->rhi", rate_heads, rate_gate, preferred_element_type=jnp.float32
    ) + jnp.einsum("rhj,hij->rhi", input_heads, input_gate, preferred_element_type=jnp.float32)
    conv_grad = (
        (conv_direct + gate_back_in.reshape(row_count, rec_width))
        .astype(jnp.bfloat16)
        .reshape(seq_count, tok_count, rec_width)
    )
    next_edge = from_behind(conv_grad[:, :margin_len, :], "ctx", -1)
    ext_grad = jnp.concatenate([conv_grad, next_edge], axis=1)
    conv_grad_f = conv_grad.astype(jnp.float32)
    branch_grad = jnp.zeros((seq_count, tok_count, rec_width), jnp.float32)
    kernel_rows = []
    for offset in range(CONV):
        branch_grad = (
            branch_grad
            + conv_kernel[offset]
            * ext_grad[:, offset : offset + tok_count].astype(jnp.float32)
            * ahead_masks[offset]
        )
        kernel_rows.append(
            jnp.sum(
                conv_grad_f
                * ext_x[:, margin_len - offset : margin_len - offset + tok_count].astype(
                    jnp.float32
                )
                * back_masks[offset],
                axis=(0, 1),
            )
        )
    grad_kernel = jnp.stack(kernel_rows)
    grad_conv = jnp.sum(conv_grad_f, axis=(0, 1))
    branch_low = branch_grad.astype(jnp.bfloat16).reshape(row_count, rec_width)
    grad_scan = matmul_lt(normed, branch_low)
    in_part = in_part + matmul_rt(branch_low, w_scan)
    in_from_norm, gain_one_part = norm_one_back(in_part)
    in_slice, gain_one_slice = (
        lax.psum_scatter(in_from_norm, "tp", scatter_dimension=1, tiled=True),
        lax.psum_scatter(gain_one_part, "tp", scatter_dimension=0, tiled=True),
    )
    grad_in = (lax.dynamic_slice_in_dim(mid_grad, col_start, part_width, 1) + in_slice).reshape(
        seq_count, tok_count, part_width
    )
    gain_two_slice = lax.dynamic_slice_in_dim(gain_two_grad, col_start, part_width, 0)
    grad_gelu_s, grad_scan_s, grad_out_s, grad_gate_s, grad_up_s, grad_down_s = (
        lax.psum_scatter(grad_gelu, ("fsdp", "ctx"), scatter_dimension=0, tiled=True),
        lax.psum_scatter(grad_scan, ("fsdp", "ctx"), scatter_dimension=0, tiled=True),
        lax.psum_scatter(grad_out, ("fsdp", "ctx"), scatter_dimension=1, tiled=True),
        lax.psum_scatter(grad_gate, ("fsdp", "ctx"), scatter_dimension=0, tiled=True),
        lax.psum_scatter(grad_up, ("fsdp", "ctx"), scatter_dimension=0, tiled=True),
        lax.psum_scatter(grad_down, ("fsdp", "ctx"), scatter_dimension=1, tiled=True),
    )
    (
        gain_one_total,
        gain_two_total,
        kernel_total,
        conv_total,
        rate_gate_total,
        input_gate_total,
        rate_bias_total,
        input_bias_total,
        decay_total,
    ) = lax.psum(
        (
            gain_one_slice,
            gain_two_slice,
            grad_kernel,
            grad_conv,
            grad_rate_gate,
            grad_input_gate,
            grad_rate_bias,
            grad_input_bias,
            grad_decay,
        ),
        ("fsdp", "ctx"),
    )
    return (
        block_out,
        grad_in,
        gain_one_total,
        gain_two_total,
        grad_gelu_s,
        grad_scan_s,
        grad_out_s,
        grad_gate_s,
        grad_up_s,
        grad_down_s,
        kernel_total,
        conv_total,
        rate_gate_total,
        input_gate_total,
        rate_bias_total,
        input_bias_total,
        decay_total,
    )


def solution(mesh):
    in_specs = (
        P("fsdp", "ctx", "tp"),
        P("fsdp", None),
        P("fsdp", "ctx", None),
        P("tp"),
        P("tp"),
        P(("fsdp", "ctx"), "tp"),
        P(("fsdp", "ctx"), "tp"),
        P("tp", ("fsdp", "ctx")),
        P(("fsdp", "ctx"), "tp"),
        P(("fsdp", "ctx"), "tp"),
        P("tp", ("fsdp", "ctx")),
        P(None, "tp"),
        P("tp"),
        P("tp", None, None),
        P("tp", None, None),
        P("tp"),
        P("tp"),
        P("tp"),
    )
    out_specs = (
        P("fsdp", "ctx", "tp"),
        P("fsdp", "ctx", "tp"),
        P("tp"),
        P("tp"),
        P(("fsdp", "ctx"), "tp"),
        P(("fsdp", "ctx"), "tp"),
        P("tp", ("fsdp", "ctx")),
        P(("fsdp", "ctx"), "tp"),
        P(("fsdp", "ctx"), "tp"),
        P("tp", ("fsdp", "ctx")),
        P(None, "tp"),
        P("tp"),
        P("tp", None, None),
        P("tp", None, None),
        P("tp"),
        P("tp"),
        P("tp"),
    )
    return jax.shard_map(shards, mesh=mesh, in_specs=in_specs, out_specs=out_specs, check_vma=False)
```

profile of v0, /device:TPU:0, one launch (start us, length us, event | category | flops | bytes accessed | tf_op | source)
XLA Modules:
  0.0 2524.0 jit_solution(14394685174451569282)
XLA Ops:
  10.7 13.5 all-gather.4
  26.8 66.3 %all-gather.14.cloned.1.call-done = bf16[4,256,2048]{2,1,0:T(8,128)(2,1)} async-done(((bf16[4,256,512]{2,1,0:T(8,128)(2,1)}), bf16[4,256,2048]{2,1,0:T(8,128)(2,1)}) %all-gather.14.cloned.1.call-update) | async-done | bytes 4194320 | tf_op jit(solution)/shard_map/all_gather | solution.py:93
  100.0 25.2 all-gather.16.cloned.1.call-done
  125.2 6.3 convolution_convert_fusion
  172.3 7.0 convert_multiply_fusion.8
  179.3 10.2 slice.580
  189.5 9.6 slice.581
  374.8 9.6 slice.635
  474.3 5.8 pad.212
  489.6 5.7 pad.229
  498.1 5.9 pad.228
  505.0 5.8 all-gather
  516.0 7.5 multiply_add_fusion.2
  527.0 9.7 multiply_convert_fusion.3
  536.7 9.1 fusion.116
  547.9 12.2 all-gather.5
  560.1 277.4 %all-reduce.73.cloned.1.call-done = f32[1024,2048]{1,0:T(8,128)} async-done(((f32[1024,2048]{1,0:T(8,128)}), f32[1024,2048]{1,0:T(8,128)}) %all-reduce.73.cloned.1.call-update) | async-done | bytes 8388624 | tf_op jit(solution)/shard_map/psum | solution.py:179
  837.5 5.9 multiply_reduce_fusion.2
  849.7 34.1 %all-gather.22.cloned.1.call-done = bf16[2048,1536]{1,0:T(8,128)(2,1)} async-done(((bf16[256,1536]{1,0:T(8,128)(2,1)}), bf16[2048,1536]{1,0:T(8,128)(2,1)}) %all-gather.22.cloned.1.call-update) | async-done | bytes 6291472 | tf_op jit(solution)/shard_map/all_gather | solution.py:101
  883.8 11.8 fusion.117
  895.7 35.6 %all-gather.24.cloned.1.call-done = bf16[2048,1536]{1,0:T(8,128)(2,1)} async-done(((bf16[256,1536]{1,0:T(8,128)(2,1)}), bf16[2048,1536]{1,0:T(8,128)(2,1)}) %all-gather.24.cloned.1.call-update) | async-done | bytes 6291472 | tf_op jit(solution)/shard_map/all_gather | solution.py:102
  931.3 11.9 fusion.118
  943.1 36.7 %all-gather.26.cloned.1.call-done = bf16[1536,2048]{1,0:T(8,128)(2,1)} async-done(((bf16[1536,256]{1,0:T(8,128)(2,1)}), bf16[1536,2048]{1,0:T(8,128)(2,1)}) %all-gather.26.cloned.1.call-update) | async-done | bytes 6291472 | tf_op jit(solution)/shard_map/all_gather | solution.py:103
  979.9 18.6 multiply_convert_fusion.1
  998.4 10.0 fusion.120
  1008.5 10.9 convolution_add_fusion.1
  1023.8 9.7 slice.657
  1033.4 9.6 slice.664
  1043.0 9.5 slice.655
  1053.1 12.8 slice.658
  1065.9 12.7 slice.665
  1078.7 12.8 slice.656
  1091.5 11.9 fusion.119
  1103.5 206.9 %all-reduce.75.cloned.1.call-done = f32[1024,2048]{1,0:T(8,128)} async-done(((f32[1024,2048]{1,0:T(8,128)}), f32[1024,2048]{1,0:T(8,128)}) %all-reduce.75.cloned.1.call-update) | async-done | bytes 8388624 | tf_op jit(solution)/shard_map/psum | solution.py:198
  1310.4 7.7 multiply_reduce_fusion
  1325.5 11.8 fusion.72
  1340.8 9.5 slice.659
  1350.4 9.6 slice.661
  1359.9 12.8 slice.660
  1372.7 12.8 slice.662
  1480.8 9.5 slice.717
  1641.5 12.8 slice.718
  1669.5 5.7 pad.260
  1695.7 24.7 rev.15
  1720.5 24.8 rev.14
  1747.6 11.8 multiply_reduce_fusion.3
  1778.6 7.5 fusion.60
  1799.5 10.8 fusion.43
  1831.7 9.1 fusion.62
  1842.2 7.3 fusion.128
  1850.9 8.0 fusion.22
  1859.0 12.5 fusion.122
  1871.8 12.6 fusion.123
  1884.4 12.2 fusion.124
  1899.4 9.0 all-reduce.66
  1908.5 26.4 %all-reduce.67 = (f32[512]{0:T(512)}, f32[512]{0:T(512)}, f32[4,704]{1,0:T(4,128)}, f32[704]{0:T(1024)}, f32[704]{0:T(1024)}, /*index=5*/f32[704]{0:T(1024)}, f32[704]{0:T(1024)}) all-reduce(f32[512]{0:T(512)S(1)} %dynamic-slice.3, f32[512]{0:T(512)S(1)} %dynamic_slice.43, ...), channel_id=1, replica_groups=mesh['fsdp'=2,'ctx'=4,'tp'=4] {'fsdp','ctx'}, use_global_device_ids=true, to_apply=%region_14.15 | all-reduce | flops 6656 | bytes 53248 | tf_op jit(solution)/shard_map/psum | solution.py:302
  1938.5 33.6 %reduce-scatter.11.cloned.1.call-done = f32[1024,512]{1,0:T(8,128)} async-done(((f32[1024,2048]{1,0:T(8,128)}), f32[1024,512]{1,0:T(8,128)}) %reduce-scatter.11.cloned.1.call-update) | async-done | bytes 2097168 | tf_op jit(solution)/shard_map/reduce_scatter | solution.py:277
  1976.2 58.8 %all-reduce.77.cloned.1.call-done = (f32[4,176,176]{2,1,0:T(8,128)}, f32[4,176,176]{2,1,0:T(8,128)}) async-done(((f32[4,176,176]{2,1,0:T(8,128)}, f32[4,176,176]{2,1,0:T(8,128)}), (f32[4,176,176]{2,1,0:T(8,128)}, f32[4,176,176]{2,1,0:T(8,128)})) %all-reduce.77.cloned.1.call-update) | async-done | bytes 991248 | tf_op jit(solution)/shard_map/psum | solution.py:302
  2034.9 62.7 %reduce-scatter.17.cloned.1.call-done = f32[704,256]{1,0:T(8,128)} async-done(((f32[704,2048]{1,0:T(8,128)}), f32[704,256]{1,0:T(8,128)}) %reduce-scatter.17.cloned.1.call-update) | async-done | bytes 720912 | tf_op jit(solution)/shard_map/reduce_scatter | solution.py:287
  2097.6 63.0 %reduce-scatter.13.cloned.1.call-done = f32[256,704]{0,1:T(8,128)} async-done(((f32[2048,704]{0,1:T(8,128)}), f32[256,704]{0,1:T(8,128)}) %reduce-scatter.13.cloned.1.call-update) | async-done | bytes 720912 | tf_op jit(solution)/shard_map/reduce_scatter | solution.py:285
  2160.6 63.3 %reduce-scatter.15.cloned.1.call-done = f32[256,704]{0,1:T(8,128)} async-done(((f32[2048,704]{0,1:T(8,128)}), f32[256,704]{0,1:T(8,128)}) %reduce-scatter.15.cloned.1.call-update) | async-done | bytes 720912 | tf_op jit(solution)/shard_map/reduce_scatter | solution.py:286
  2223.9 96.3 %reduce-scatter.19.cloned.1.call-done = f32[256,1536]{1,0:T(8,128)} async-done(((f32[2048,1536]{1,0:T(8,128)}), f32[256,1536]{1,0:T(8,128)}) %reduce-scatter.19.cloned.1.call-update) | async-done | bytes 1572880 | tf_op jit(solution)/shard_map/reduce_scatter | solution.py:288
  2320.2 96.3 %reduce-scatter.21.cloned.1.call-done = f32[256,1536]{1,0:T(8,128)} async-done(((f32[2048,1536]{1,0:T(8,128)}), f32[256,1536]{1,0:T(8,128)}) %reduce-scatter.21.cloned.1.call-update) | async-done | bytes 1572880 | tf_op jit(solution)/shard_map/reduce_scatter | solution.py:289
  2416.5 96.4 %reduce-scatter.23.cloned.1.call-done = f32[1536,256]{1,0:T(8,128)} async-done(((f32[1536,2048]{1,0:T(8,128)}), f32[1536,256]{1,0:T(8,128)}) %reduce-scatter.23.cloned.1.call-update) | async-done | bytes 1572880 | tf_op jit(solution)/shard_map/reduce_scatter | solution.py:290
  (599 shorter events, 724.4 us)
Async XLA Ops:
  7.2 141.0 %copy-start = (bf16[4,176,176]{2,1,0:T(8,128)(2,1)S(1)}, bf16[4,176,176]{2,1,0:T(8,128)(2,1)}, u32[]{:S(2)}) copy-start(bf16[4,176,176]{2,1,0:T(8,128)(2,1)} %param.35) | copy-start | bytes 743428
  7.2 85.9 %all-gather.14.cloned.1.call-start = ((), (), s32[]{:S(2)}) async-start(), calls=%async_computation.8 | async-start | bytes 5242880 | tf_op jit(solution)/shard_map/all_gather | solution.py:93
  7.9 117.3 %all-gather.16.cloned.1.call-start = ((), (), s32[]{:S(2)}) async-start(), calls=%async_computation.9 | async-start | bytes 3244032 | tf_op jit(solution)/shard_map/all_gather | solution.py:99
  8.7 518.3 %all-gather.18.cloned.1.call-start = ((), (), s32[]{:S(2)}) async-start(), calls=%async_computation.10 | async-start | bytes 3244032 | tf_op jit(solution)/shard_map/all_gather | solution.py:98
  9.4 527.2 %all-gather.20.cloned.1.call-start = ((), (), s32[]{:S(2)}) async-start(), calls=%async_computation.11 | async-start | bytes 3244032 | tf_op jit(solution)/shard_map/all_gather | solution.py:100
  10.0 827.5 %all-reduce.73.cloned.1.call-start = ((), (), s32[]{:S(2)}) async-start(), calls=%async_computation.12 | async-start | bytes 16777216 | tf_op jit(solution)/shard_map/psum | solution.py:179
  24.3 75.8 %copy-start.51 = (f32[4,1,512]{2,1,0:T(1,128)}, f32[4,1,512]{2,1,0:T(1,128)S(1)}, u32[]{:S(2)}) copy-start(f32[4,1,512]{2,1,0:T(1,128)S(1)} %convert_element_type.180) | copy-start | bytes 24580
  25.2 113.3 %copy-start.71 = (f32[704]{0:T(1024)}, f32[704]{0:T(1024)S(1)}, u32[]{:S(2)}) copy-start(f32[704]{0:T(1024)S(1)} %get-tuple-element.255) | copy-start | bytes 8452
  25.2 113.3 %copy-start.73 = (f32[704]{0:T(1024)}, f32[704]{0:T(1024)S(1)}, u32[]{:S(2)}) copy-start(f32[704]{0:T(1024)S(1)} %get-tuple-element.256) | copy-start | bytes 8452
  25.2 113.3 %copy-start.75 = (f32[704]{0:T(1024)}, f32[704]{0:T(1024)S(1)}, u32[]{:S(2)}) copy-start(f32[704]{0:T(1024)S(1)} %get-tuple-element.257) | copy-start | bytes 8452
  25.2 113.3 %copy-start.77 = (f32[704]{0:T(1024)}, f32[704]{0:T(1024)S(1)}, u32[]{:S(2)}) copy-start(f32[704]{0:T(1024)S(1)} %get-tuple-element.258) | copy-start | bytes 8452
  25.9 993.5 %copy-start.49 = (f32[704]{0:T(1024)}, f32[704]{0:T(1024)S(1)}, u32[]{:S(2)}) copy-start(f32[704]{0:T(1024)S(1)} %fusion.94) | copy-start | bytes 8452
  132.6 6.9 copy-start.102
  134.1 4.3 collective-permute-start
  137.2 8.0 copy-start.79
  137.2 8.0 copy-start.81
  137.2 35.1 %copy-start.47 = (f32[4,256]{1,0:T(4,128)}, f32[4,256]{1,0:T(4,128)S(1)}, u32[]{:S(2)}) copy-start(f32[4,256]{1,0:T(4,128)S(1)} %get-tuple-element.377) | copy-start | bytes 12292
  138.4 9.7 copy-start.11
  158.1 14.2 copy-start.4
  179.3 19.8 copy-start.6
  301.5 37.3 %copy-start.67 = (f32[4,1,704]{2,1,0:T(1,128)S(1)}, f32[4,1,704]{2,1,0:T(1,128)}, u32[]{:S(2)}) copy-start(f32[4,1,704]{2,1,0:T(1,128)} %slice.752) | copy-start | bytes 33796
  403.2 6.3 copy-start.70
  545.8 338.1 %all-gather.22.cloned.1.call-start = ((), (), s32[]{:S(2)}) async-start(), calls=%async_computation.13 | async-start | bytes 7077888 | tf_op jit(solution)/shard_map/all_gather | solution.py:101
  546.4 384.9 %all-gather.24.cloned.1.call-start = ((), (), s32[]{:S(2)}) async-start(), calls=%async_computation.14 | async-start | bytes 7077888 | tf_op jit(solution)/shard_map/all_gather | solution.py:102
  547.1 432.8 %all-gather.26.cloned.1.call-start = ((), (), s32[]{:S(2)}) async-start(), calls=%async_computation.15 | async-start | bytes 7077888 | tf_op jit(solution)/shard_map/all_gather | solution.py:103
  547.9 762.5 %all-reduce.75.cloned.1.call-start = ((), (), s32[]{:S(2)}) async-start(), calls=%async_computation.17 | async-start | bytes 16777216 | tf_op jit(solution)/shard_map/psum | solution.py:198
  560.1 750.3 %copy-start.42 = (f32[4,1,512]{2,1,0:T(1,128)}, f32[4,1,512]{2,1,0:T(1,128)S(1)}, u32[]{:S(2)}) copy-start(f32[4,1,512]{2,1,0:T(1,128)S(1)} %convert_element_type.181) | copy-start | bytes 24580
  843.4 467.0 %copy-start.53 = (f32[1024]{0:T(1024)}, f32[1024]{0:T(1024)S(1)}, u32[]{:S(2)}) copy-start(f32[1024]{0:T(1024)S(1)} %fusion.101) | copy-start | bytes 12292
  998.4 10.0 copy-start.112
  998.4 10.0 copy-start.105
  1019.4 915.5 %reduce-scatter.9.cloned.1.call-start = ((), (), s32[]{:S(2)}) async-start(), calls=%async_computation.16 | async-start | bytes 10485760 | tf_op jit(solution)/shard_map/reduce_scatter | solution.py:187
  1103.4 868.7 %reduce-scatter.11.cloned.1.call-start = ((), (), s32[]{:S(2)}) async-start(), calls=%async_computation.18 | async-start | bytes 10485760 | tf_op jit(solution)/shard_map/reduce_scatter | solution.py:277
  1310.4 9.0 copy-start.9
  1310.4 10.2 copy-start.30
  1325.5 11.8 copy-start.15
  1523.2 30.4 %copy-start.66 = (f32[4,1,704]{2,1,0:T(1,128)S(1)}, f32[4,1,704]{2,1,0:T(1,128)}, u32[]{:S(2)}) copy-start(f32[4,1,704]{2,1,0:T(1,128)} %slice.804) | copy-start | bytes 33796
  1531.5 30.1 %copy-start.65 = (f32[4,1,704]{2,1,0:T(1,128)S(1)}, f32[4,1,704]{2,1,0:T(1,128)}, u32[]{:S(2)}) copy-start(f32[4,1,704]{2,1,0:T(1,128)} %slice.829) | copy-start | bytes 33796
  1566.9 10.0 copy-start.69
  1574.4 15.6 copy-start.68
  1615.5 5.7 copy-start.62
  1654.3 5.5 copy-start.61
  1675.2 5.1 copy-start.20
  1675.2 5.4 copy-start.21
  1720.4 24.9 copy-start.39
  1720.4 27.1 %copy-start.5 = (f32[4,256,704]{2,1,0:T(8,128)S(1)}, f32[4,256,704]{2,1,0:T(8,128)}, u32[]{:S(2)}) copy-start(f32[4,256,704]{2,1,0:T(8,128)} %copy-done.4) | copy-start | bytes 8650756
  1720.4 27.1 %copy-start.48 = (f32[4,256]{1,0:T(4,128)S(1)}, f32[4,256]{1,0:T(4,128)}, u32[]{:S(2)}) copy-start(f32[4,256]{1,0:T(4,128)} %copy-done.47) | copy-start | bytes 12292
  1720.4 27.2 %copy-start.50 = (f32[704]{0:T(1024)S(1)}, f32[704]{0:T(1024)}, u32[]{:S(2)}) copy-start(f32[704]{0:T(1024)} %copy-done.49) | copy-start | bytes 8452
  1720.4 27.2 %copy-start.56 = (f32[704]{0:T(1024)S(1)}, f32[704]{0:T(1024)}, u32[]{:S(2)}) copy-start(f32[704]{0:T(1024)} %param.38) | copy-start | bytes 8452
  1720.5 27.2 %copy-start.59 = (f32[704]{0:T(1024)S(1)}, f32[704]{0:T(1024)}, u32[]{:S(2)}) copy-start(f32[704]{0:T(1024)} %param.37) | copy-start | bytes 8452
  1720.5 27.2 %copy-start.60 = (f32[4,1,704]{2,1,0:T(1,128)S(1)}, f32[4,1,704]{2,1,0:T(1,128)}, u32[]{:S(2)}) copy-start(f32[4,1,704]{2,1,0:T(1,128)} %broadcast_in_dim.10) | copy-start | bytes 33796
  1799.4 12.1 copy-start.107
  1799.5 12.1 copy-start.110
  1810.3 5.0 collective-permute-start.1
  1811.7 6.1 copy-start.3
  1826.9 208.0 %all-reduce.77.cloned.1.call-start = ((), (), s32[]{:S(2)}) async-start(), calls=%async_computation.25 | async-start | bytes 2883584 | tf_op jit(solution)/shard_map/psum | solution.py:302
  1831.7 265.9 %reduce-scatter.17.cloned.1.call-start = ((), (), s32[]{:S(2)}) async-start(), calls=%async_computation.21 | async-start | bytes 6488064 | tf_op jit(solution)/shard_map/reduce_scatter | solution.py:287
  1840.8 319.8 %reduce-scatter.13.cloned.1.call-start = ((), (), s32[]{:S(2)}) async-start(), calls=%async_computation.19 | async-start | bytes 6488064 | tf_op jit(solution)/shard_map/reduce_scatter | solution.py:285
  1849.5 374.4 %reduce-scatter.15.cloned.1.call-start = ((), (), s32[]{:S(2)}) async-start(), calls=%async_computation.20 | async-start | bytes 6488064 | tf_op jit(solution)/shard_map/reduce_scatter | solution.py:286
  1858.9 461.3 %reduce-scatter.19.cloned.1.call-start = ((), (), s32[]{:S(2)}) async-start(), calls=%async_computation.22 | async-start | bytes 14155776 | tf_op jit(solution)/shard_map/reduce_scatter | solution.py:288
  1871.5 545.0 %reduce-scatter.21.cloned.1.call-start = ((), (), s32[]{:S(2)}) async-start(), calls=%async_computation.23 | async-start | bytes 14155776 | tf_op jit(solution)/shard_map/reduce_scatter | solution.py:289
  1884.3 628.6 %reduce-scatter.23.cloned.1.call-start = ((), (), s32[]{:S(2)}) async-start(), calls=%async_computation.24 | async-start | bytes 14155776 | tf_op jit(solution)/shard_map/reduce_scatter | solution.py:290
  1896.7 11.8 copy-start.95
  1896.7 11.8 copy-start.96
  1896.7 11.8 copy-start.97
  (69 other events, 214.7 us)
Sparse Core Ops, SparseCore 0:
  9.6 83.4 all-gather.13
  95.0 30.1 all-gather.15
  127.1 31.8 all-gather.17
  160.7 31.6 all-gather.19
  545.9 291.5 all-reduce.72
  839.3 44.5 all-gather.21
  885.7 45.5 all-gather.23
  933.2 46.6 all-gather.25
  1019.5 290.8 all-reduce.74
  1312.6 143.4 reduce-scatter.8
  1827.0 145.0 reduce-scatter.10
  1975.8 59.0 all-reduce.76
  2039.3 58.2 reduce-scatter.16
  2101.5 59.0 reduce-scatter.12
  2164.8 58.9 reduce-scatter.14
  2227.8 92.3 reduce-scatter.18
  2324.1 92.3 reduce-scatter.20
  2420.5 92.3 reduce-scatter.22
where the time goes:
time: 2550 us; the launch traced here: 2520 us
  waiting for transfers between devices  1260 us (49%)
  local copies, waits for them, and re-layouts  706 us (28%)
  other arithmetic  262 us (10%)
  matrix products  194 us (8%)
  blocking collectives  83 us (3%)
    psum x1, waiting for transfers between devices, shards(): rec_total = lax.psum(rec_part, 'tp')  277 us
    slice x57, local copies, waits for them, and re-layouts, shards(): lax.associative_scan(combine, (next_coef, state_direct), reverse=True, ax...  215 us
    psum x1, waiting for transfers between devices, shards(): mid_norm_grad = lax.psum(mid_part, 'tp')  207 us
    slice x52, local copies, waits for them, and re-layouts, shards(): lax.associative_scan(combine, (coeffs, inputs), axis=1)  128 us
    pad x28, local copies, waits for them, and re-layouts, shards(): lax.associative_scan(combine, (coeffs, inputs), axis=1)  110 us
    pad x28, local copies, waits for them, and re-layouts, shards(): lax.associative_scan(combine, (next_coef, state_direct), reverse=True, ax...  108 us
    reduce_scatter x1, waiting for transfers between devices, shards(): lax.psum_scatter(grad_down, ('fsdp', 'ctx'), scatter_dimension=1, tiled=T...  96.4 us
    reduce_scatter x1, waiting for transfers between devices, shards(): lax.psum_scatter(grad_up, ('fsdp', 'ctx'), scatter_dimension=0, tiled=True)  96.3 us
  transfers between devices with their start and end apart: 20, of which 15 were waited for; matrix products, arithmetic and copies ran while one was open for 43% of the time, Pallas kernels for 0%

commit v1 on v0

--- a/solution.py
+++ b/solution.py
@@ -176,7 +176,7 @@
     mixed_in = (state_rows * y_act).astype(jnp.bfloat16)
     rec_part = matmul(mixed_in, w_out)
     col_start = lax.axis_index("tp") * part_width
-    rec_total = lax.psum(rec_part, "tp")
+    rec_total = jnp.sum(lax.all_gather(rec_part, "tp"), axis=0)
     mid_rows = x_rows + rec_total
     normed_mid_f, norm_two_back = jax.vjp(rms_scale, mid_rows, gain_two.astype(jnp.float32))
     normed_mid = normed_mid_f.astype(jnp.bfloat16)

time: 2550 us -> 2830 us (1.11)
  waiting for transfers between devices: 1260 us -> 1510 us
    all_gather x0 -> x1, waiting for transfers between devices: none -> 548 us  [shards(): rec_total = jnp.sum(lax.all_gather(rec_part, 'tp'), axis=0)]
    psum x1 -> x0, waiting for transfers between devices: 277 us -> none  [shards(): rec_total = lax.psum(rec_part, 'tp')]
  transfers between devices with their start and end apart: 20 -> 20, of which waited for: 15 -> 15; matrix products, arithmetic and copies ran while one was open for 43% -> 40% of each run, Pallas kernels for 0% -> 0%
where the time goes in v1:
time: 2830 us; the launch traced here: 2800 us
  waiting for transfers between devices  1510 us (53%)
  local copies, waits for them, and re-layouts  710 us (25%)
  other arithmetic  284 us (10%)
  matrix products  192 us (7%)
  blocking collectives  83.2 us (3%)
    all_gather x1, waiting for transfers between devices, shards(): rec_total = jnp.sum(lax.all_gather(rec_part, 'tp'), axis=0)  548 us
    slice x57, local copies, waits for them, and re-layouts, shards(): lax.associative_scan(combine, (next_coef, state_direct), reverse=True, ax...  216 us
    psum x1, waiting for transfers between devices, shards(): mid_norm_grad = lax.psum(mid_part, 'tp')  207 us
    slice x52, local copies, waits for them, and re-layouts, shards(): lax.associative_scan(combine, (coeffs, inputs), axis=1)  127 us
    pad x28, local copies, waits for them, and re-layouts, shards(): lax.associative_scan(combine, (next_coef, state_direct), reverse=True, ax...  111 us
    pad x28, local copies, waits for them, and re-layouts, shards(): lax.associative_scan(combine, (coeffs, inputs), axis=1)  110 us
    reduce_scatter x1, waiting for transfers between devices, shards(): lax.psum_scatter(grad_down, ('fsdp', 'ctx'), scatter_dimension=1, tiled=T...  96.4 us
    reduce_scatter x1, waiting for transfers between devices, shards(): lax.psum_scatter(grad_up, ('fsdp', 'ctx'), scatter_dimension=0, tiled=True)  96.3 us
  transfers between devices with their start and end apart: 20, of which 15 were waited for; matrix products, arithmetic and copies ran while one was open for 40% of the time, Pallas kernels for 0%

profile of v1, /device:TPU:0, one launch (start us, length us, event | category | flops | bytes accessed | tf_op | source)
XLA Modules:
  0.0 2798.3 jit_solution(9545518365970534735)
XLA Ops:
  10.7 13.5 all-gather.5
  26.8 66.3 %all-gather.16.cloned.1.call-done = bf16[4,256,2048]{2,1,0:T(8,128)(2,1)} async-done(((bf16[4,256,512]{2,1,0:T(8,128)(2,1)}), bf16[4,256,2048]{2,1,0:T(8,128)(2,1)}) %all-gather.16.cloned.1.call-update) | async-done | bytes 4194320 | tf_op jit(solution)/shard_map/all_gather | solution.py:93
  100.0 25.2 all-gather.18.cloned.1.call-done
  125.2 6.3 convolution_convert_fusion
  172.1 7.0 convert_multiply_fusion.8
  179.1 10.1 slice.580
  189.2 9.5 slice.581
  373.5 9.6 slice.635
  480.1 5.9 all-gather.1
  504.0 5.9 all-gather
  515.2 7.1 multiply_add_fusion.2
  525.9 9.6 multiply_convert_fusion.3
  535.6 9.0 fusion.117
  546.8 11.9 all-gather.6
  558.7 548.1 %all-gather.30.cloned.1.call-done = f32[4096,2048]{1,0:T(8,128)} async-done(((f32[1024,2048]{1,0:T(8,128)}), f32[4096,2048]{1,0:T(8,128)}) %all-gather.30.cloned.1.call-update) | async-done | bytes 33554448 | tf_op jit(solution)/shard_map/all_gather | solution.py:179
  1106.9 16.9 reduce_sum.135
  1123.8 5.9 fusion.9
  1132.3 6.0 multiply_convert_fusion
  1138.2 14.1 all-gather.24.cloned.1.call-done
  1152.3 11.7 fusion.118
  1164.1 35.7 %all-gather.26.cloned.1.call-done = bf16[2048,1536]{1,0:T(8,128)(2,1)} async-done(((bf16[256,1536]{1,0:T(8,128)(2,1)}), bf16[2048,1536]{1,0:T(8,128)(2,1)}) %all-gather.26.cloned.1.call-update) | async-done | bytes 6291472 | tf_op jit(solution)/shard_map/all_gather | solution.py:102
  1199.8 11.7 fusion.119
  1211.5 36.9 %all-gather.28.cloned.1.call-done = bf16[1536,2048]{1,0:T(8,128)(2,1)} async-done(((bf16[1536,256]{1,0:T(8,128)(2,1)}), bf16[1536,2048]{1,0:T(8,128)(2,1)}) %all-gather.28.cloned.1.call-update) | async-done | bytes 6291472 | tf_op jit(solution)/shard_map/all_gather | solution.py:103
  1248.4 18.8 multiply_convert_fusion.1
  1267.2 10.0 fusion.121
  1277.2 10.5 convolution_add_fusion.1
  1292.6 9.6 slice.657
  1302.3 9.5 slice.664
  1311.8 9.5 slice.655
  1322.0 12.8 slice.658
  1334.8 12.7 slice.665
  1347.5 12.8 slice.656
  1360.3 11.7 fusion.120
  1372.1 206.6 %all-reduce.72.cloned.1.call-done = f32[1024,2048]{1,0:T(8,128)} async-done(((f32[1024,2048]{1,0:T(8,128)}), f32[1024,2048]{1,0:T(8,128)}) %all-reduce.72.cloned.1.call-update) | async-done | bytes 8388624 | tf_op jit(solution)/shard_map/psum | solution.py:198
  1578.7 8.8 multiply_reduce_fusion
  1590.2 6.4 fusion.2
  1596.6 10.4 fusion.74
  1610.5 9.5 slice.659
  1620.0 9.6 slice.661
  1629.6 12.8 slice.660
  1642.4 12.9 slice.662
  1752.0 9.5 slice.717
  1916.4 12.9 slice.718
  1970.6 24.7 rev.15
  1995.3 24.9 rev.14
  2022.6 11.9 multiply_reduce_fusion.2
  2053.5 7.5 fusion.62
  2074.1 10.9 fusion.45
  2106.3 9.0 fusion.64
  2116.8 7.1 fusion.129
  2125.2 8.1 fusion.24
  2133.4 12.5 fusion.123
  2146.2 12.6 fusion.124
  2158.9 12.3 fusion.125
  2173.9 9.0 all-reduce.66
  2183.1 26.4 all-reduce.67
  2213.1 33.4 %reduce-scatter.11.cloned.1.call-done = f32[1024,512]{1,0:T(8,128)} async-done(((f32[1024,2048]{1,0:T(8,128)}), f32[1024,512]{1,0:T(8,128)}) %reduce-scatter.11.cloned.1.call-update) | async-done | bytes 2097168 | tf_op jit(solution)/shard_map/reduce_scatter | solution.py:277
  2250.5 58.8 %all-reduce.74.cloned.1.call-done = (f32[4,176,176]{2,1,0:T(8,128)}, f32[4,176,176]{2,1,0:T(8,128)}) async-done(((f32[4,176,176]{2,1,0:T(8,128)}, f32[4,176,176]{2,1,0:T(8,128)}), (f32[4,176,176]{2,1,0:T(8,128)}, f32[4,176,176]{2,1,0:T(8,128)})) %all-reduce.74.cloned.1.call-update) | async-done | bytes 991248 | tf_op jit(solution)/shard_map/psum | solution.py:302
  2309.3 62.7 %reduce-scatter.17.cloned.1.call-done = f32[704,256]{1,0:T(8,128)} async-done(((f32[704,2048]{1,0:T(8,128)}), f32[704,256]{1,0:T(8,128)}) %reduce-scatter.17.cloned.1.call-update) | async-done | bytes 720912 | tf_op jit(solution)/shard_map/reduce_scatter | solution.py:287
  2371.9 63.0 %reduce-scatter.13.cloned.1.call-done = f32[256,704]{0,1:T(8,128)} async-done(((f32[2048,704]{0,1:T(8,128)}), f32[256,704]{0,1:T(8,128)}) %reduce-scatter.13.cloned.1.call-update) | async-done | bytes 720912 | tf_op jit(solution)/shard_map/reduce_scatter | solution.py:285
  2434.9 63.3 %reduce-scatter.15.cloned.1.call-done = f32[256,704]{0,1:T(8,128)} async-done(((f32[2048,704]{0,1:T(8,128)}), f32[256,704]{0,1:T(8,128)}) %reduce-scatter.15.cloned.1.call-update) | async-done | bytes 720912 | tf_op jit(solution)/shard_map/reduce_scatter | solution.py:286
  2498.2 96.3 %reduce-scatter.19.cloned.1.call-done = f32[256,1536]{1,0:T(8,128)} async-done(((f32[2048,1536]{1,0:T(8,128)}), f32[256,1536]{1,0:T(8,128)}) %reduce-scatter.19.cloned.1.call-update) | async-done | bytes 1572880 | tf_op jit(solution)/shard_map/reduce_scatter | solution.py:288
  2594.5 96.3 %reduce-scatter.21.cloned.1.call-done = f32[256,1536]{1,0:T(8,128)} async-done(((f32[2048,1536]{1,0:T(8,128)}), f32[256,1536]{1,0:T(8,128)}) %reduce-scatter.21.cloned.1.call-update) | async-done | bytes 1572880 | tf_op jit(solution)/shard_map/reduce_scatter | solution.py:289
  2690.9 96.4 %reduce-scatter.23.cloned.1.call-done = f32[1536,256]{1,0:T(8,128)} async-done(((f32[1536,2048]{1,0:T(8,128)}), f32[1536,256]{1,0:T(8,128)}) %reduce-scatter.23.cloned.1.call-update) | async-done | bytes 1572880 | tf_op jit(solution)/shard_map/reduce_scatter | solution.py:290
  (603 shorter events, 737.4 us)
Async XLA Ops:
  7.2 140.6 %copy-start = (bf16[4,176,176]{2,1,0:T(8,128)(2,1)S(1)}, bf16[4,176,176]{2,1,0:T(8,128)(2,1)}, u32[]{:S(2)}) copy-start(bf16[4,176,176]{2,1,0:T(8,128)(2,1)} %param.35) | copy-start | bytes 743428
  7.2 85.9 %all-gather.16.cloned.1.call-start = ((), (), s32[]{:S(2)}) async-start(), calls=%async_computation.8 | async-start | bytes 5242880 | tf_op jit(solution)/shard_map/all_gather | solution.py:93
  7.9 117.3 %all-gather.18.cloned.1.call-start = ((), (), s32[]{:S(2)}) async-start(), calls=%async_computation.9 | async-start | bytes 3244032 | tf_op jit(solution)/shard_map/all_gather | solution.py:99
  8.7 517.2 %all-gather.20.cloned.1.call-start = ((), (), s32[]{:S(2)}) async-start(), calls=%async_computation.10 | async-start | bytes 3244032 | tf_op jit(solution)/shard_map/all_gather | solution.py:98
  9.4 526.1 %all-gather.22.cloned.1.call-start = ((), (), s32[]{:S(2)}) async-start(), calls=%async_computation.11 | async-start | bytes 3244032 | tf_op jit(solution)/shard_map/all_gather | solution.py:100
  10.0 1096.9 %all-gather.30.cloned.1.call-start = ((), (), s32[]{:S(2)}) async-start(), calls=%async_computation.24 | async-start | bytes 41943040 | tf_op jit(solution)/shard_map/all_gather | solution.py:179
  24.3 75.7 %copy-start.46 = (f32[4,1,512]{2,1,0:T(1,128)}, f32[4,1,512]{2,1,0:T(1,128)S(1)}, u32[]{:S(2)}) copy-start(f32[4,1,512]{2,1,0:T(1,128)S(1)} %convert_element_type.181) | copy-start | bytes 24580
  25.2 113.3 %copy-start.66 = (f32[704]{0:T(1024)}, f32[704]{0:T(1024)S(1)}, u32[]{:S(2)}) copy-start(f32[704]{0:T(1024)S(1)} %get-tuple-element.255) | copy-start | bytes 8452
  25.2 113.3 %copy-start.68 = (f32[704]{0:T(1024)}, f32[704]{0:T(1024)S(1)}, u32[]{:S(2)}) copy-start(f32[704]{0:T(1024)S(1)} %get-tuple-element.256) | copy-start | bytes 8452
  25.2 113.3 %copy-start.70 = (f32[704]{0:T(1024)}, f32[704]{0:T(1024)S(1)}, u32[]{:S(2)}) copy-start(f32[704]{0:T(1024)S(1)} %get-tuple-element.257) | copy-start | bytes 8452
  25.2 113.3 %copy-start.72 = (f32[704]{0:T(1024)}, f32[704]{0:T(1024)S(1)}, u32[]{:S(2)}) copy-start(f32[704]{0:T(1024)S(1)} %get-tuple-element.258) | copy-start | bytes 8452
  25.9 146.1 %copy-start.43 = (f32[704]{0:T(1024)}, f32[704]{0:T(1024)S(1)}, u32[]{:S(2)}) copy-start(f32[704]{0:T(1024)S(1)} %fusion.96) | copy-start | bytes 8452
  132.6 6.5 copy-start.99
  134.1 4.3 collective-permute-start
  137.2 7.6 copy-start.74
  137.2 7.6 copy-start.76
  137.2 34.9 %copy-start.41 = (f32[4,256]{1,0:T(4,128)}, f32[4,256]{1,0:T(4,128)S(1)}, u32[]{:S(2)}) copy-start(f32[4,256]{1,0:T(4,128)S(1)} %get-tuple-element.377) | copy-start | bytes 12292
  138.4 9.4 copy-start.12
  157.8 14.2 copy-start.5
  179.1 19.6 copy-start.7
  296.0 42.3 %copy-start.62 = (f32[4,1,704]{2,1,0:T(1,128)S(1)}, f32[4,1,704]{2,1,0:T(1,128)}, u32[]{:S(2)}) copy-start(f32[4,1,704]{2,1,0:T(1,128)} %slice.752) | copy-start | bytes 33796
  401.9 6.3 copy-start.65
  544.6 607.7 %all-gather.24.cloned.1.call-start = ((), (), s32[]{:S(2)}) async-start(), calls=%async_computation.12 | async-start | bytes 7077888 | tf_op jit(solution)/shard_map/all_gather | solution.py:101
  545.2 654.6 %all-gather.26.cloned.1.call-start = ((), (), s32[]{:S(2)}) async-start(), calls=%async_computation.13 | async-start | bytes 7077888 | tf_op jit(solution)/shard_map/all_gather | solution.py:102
  546.0 702.4 %all-gather.28.cloned.1.call-start = ((), (), s32[]{:S(2)}) async-start(), calls=%async_computation.14 | async-start | bytes 7077888 | tf_op jit(solution)/shard_map/all_gather | solution.py:103
  546.7 1032.0 %all-reduce.72.cloned.1.call-start = ((), (), s32[]{:S(2)}) async-start(), calls=%async_computation.16 | async-start | bytes 16777216 | tf_op jit(solution)/shard_map/psum | solution.py:198
  1123.8 5.9 copy-start.2
  1123.8 8.5 copy-start.4
  1129.7 8.6 copy-start.82
  1267.2 10.0 copy-start.110
  1267.2 10.0 copy-start.102
  1287.7 921.7 %reduce-scatter.9.cloned.1.call-start = ((), (), s32[]{:S(2)}) async-start(), calls=%async_computation.15 | async-start | bytes 10485760 | tf_op jit(solution)/shard_map/reduce_scatter | solution.py:187
  1372.0 874.4 %reduce-scatter.11.cloned.1.call-start = ((), (), s32[]{:S(2)}) async-start(), calls=%async_computation.17 | async-start | bytes 10485760 | tf_op jit(solution)/shard_map/reduce_scatter | solution.py:277
  1578.7 8.8 slice-start
  1578.7 8.8 copy-start.83
  1578.7 9.1 slice-start.1
  1578.7 11.5 copy-start.10
  1590.2 6.4 copy-start.34
  1590.2 6.4 copy-start.105
  1780.9 37.1 %copy-start.61 = (f32[4,1,704]{2,1,0:T(1,128)S(1)}, f32[4,1,704]{2,1,0:T(1,128)}, u32[]{:S(2)}) copy-start(f32[4,1,704]{2,1,0:T(1,128)} %slice.830) | copy-start | bytes 33796
  1790.0 38.4 %copy-start.60 = (f32[4,1,704]{2,1,0:T(1,128)S(1)}, f32[4,1,704]{2,1,0:T(1,128)}, u32[]{:S(2)}) copy-start(f32[4,1,704]{2,1,0:T(1,128)} %slice.804) | copy-start | bytes 33796
  1806.3 30.1 %copy-start.59 = (f32[4,1,704]{2,1,0:T(1,128)S(1)}, f32[4,1,704]{2,1,0:T(1,128)}, u32[]{:S(2)}) copy-start(f32[4,1,704]{2,1,0:T(1,128)} %slice.829) | copy-start | bytes 33796
  1841.8 10.0 copy-start.64
  1849.2 15.5 copy-start.63
  1995.3 27.3 copy-start.6
  1995.3 27.3 copy-start.42
  1995.3 27.3 copy-start.45
  1995.3 27.3 copy-start.50
  1995.3 27.3 copy-start.53
  1995.3 27.3 copy-start.54
  2074.1 12.2 copy-start.104
  2074.1 12.2 copy-start.108
  2085.0 5.0 collective-permute-start.1
  2086.4 6.1 copy-start.3
  2101.5 207.7 %all-reduce.74.cloned.1.call-start = ((), (), s32[]{:S(2)}) async-start(), calls=%async_computation.25 | async-start | bytes 2883584 | tf_op jit(solution)/shard_map/psum | solution.py:302
  2106.3 265.6 %reduce-scatter.17.cloned.1.call-start = ((), (), s32[]{:S(2)}) async-start(), calls=%async_computation.20 | async-start | bytes 6488064 | tf_op jit(solution)/shard_map/reduce_scatter | solution.py:287
  2115.4 319.5 %reduce-scatter.13.cloned.1.call-start = ((), (), s32[]{:S(2)}) async-start(), calls=%async_computation.18 | async-start | bytes 6488064 | tf_op jit(solution)/shard_map/reduce_scatter | solution.py:285
  2123.9 374.3 %reduce-scatter.15.cloned.1.call-start = ((), (), s32[]{:S(2)}) async-start(), calls=%async_computation.19 | async-start | bytes 6488064 | tf_op jit(solution)/shard_map/reduce_scatter | solution.py:286
  2133.4 461.1 %reduce-scatter.19.cloned.1.call-start = ((), (), s32[]{:S(2)}) async-start(), calls=%async_computation.21 | async-start | bytes 14155776 | tf_op jit(solution)/shard_map/reduce_scatter | solution.py:288
  2145.9 544.9 %reduce-scatter.21.cloned.1.call-start = ((), (), s32[]{:S(2)}) async-start(), calls=%async_computation.22 | async-start | bytes 14155776 | tf_op jit(solution)/shard_map/reduce_scatter | solution.py:289
  2158.8 628.4 %reduce-scatter.23.cloned.1.call-start = ((), (), s32[]{:S(2)}) async-start(), calls=%async_computation.23 | async-start | bytes 14155776 | tf_op jit(solution)/shard_map/reduce_scatter | solution.py:290
  2171.2 11.9 copy-start.92
  2171.2 11.9 copy-start.93
  2171.2 11.8 copy-start.94
  (69 other events, 223.1 us)
Sparse Core Ops, SparseCore 0:
  9.6 83.4 all-gather.15
  95.0 30.1 all-gather.17
  127.1 31.8 all-gather.19
  160.7 31.6 all-gather.21
  544.8 562.0 all-gather.29
  1108.6 43.6 all-gather.23
  1154.2 45.5 all-gather.25
  1201.7 46.6 all-gather.27
  1287.9 290.8 all-reduce.71
  1580.9 143.4 reduce-scatter.8
  2101.6 144.7 reduce-scatter.10
  2250.1 59.0 all-reduce.73
  2313.7 58.2 reduce-scatter.16
  2375.8 59.0 reduce-scatter.12
  2439.1 58.9 reduce-scatter.14
  2502.1 92.3 reduce-scatter.18
  2598.4 92.3 reduce-scatter.20
  2694.8 92.3 reduce-scatter.22
